TPU v7x, 512 devices: a whole 4x4x16 slice. The times are simulated.
512 devices in a mesh: view: 16 (over z_lo, y), tile: 32 (over x, z_hi, core).
Axes of the slice: x: 4, y: 4, z: 16 (z_hi: 4, z_lo: 4; z = z_hi * 4 + z_lo), core: 2. Of those that a mesh axis runs over, the one named last changes fastest.
Arguments:
- estimate: float32 [256, 256, 128], P('tile', 'view'), may hold values from 0.5 to 1.5
- images: float32 [16, 256, 256, 128], P('view', 'tile'), may hold values from 0.25 to 4
- taps_first: float32 [16, 5], P('view'), may hold values from 0.1 to 1
- taps_second: float32 [16, 7], P('view'), may hold values from 0.1 to 1
- taps_axial: float32 [16, 33], P('view'), may hold values from 0.02 to 0.2
Outputs:
- deconvolved: float32 [256, 256, 128], P('tile', 'view')
All inputs are finite; a program needn't handle non-finite values.
Results may differ from a plain program's by a relative error of at most 0.0001.
Values sent between devices are 32-bit elements; how exact they have to be, the bound alone decides.
No kernel may reach another device: no remote copies, remote signals or barrier semaphores. Data moves between devices by JAX's collectives and lax.ppermute only.
A program may use at most 64 MiB of HBM per device.

v0:
```python
import jax
import jax.numpy as jnp
from jax import lax
from jax.sharding import PartitionSpec as P

ITERS = 2


def extended(cells, sides, width):
    for axis, dim in sides:
        count = lax.axis_size(axis)
        ends = count - 1
        head = lax.slice_in_dim(cells, 0, width, axis=dim)
        tail = lax.slice_in_dim(cells, cells.shape[dim] - width, cells.shape[dim], axis=dim)
        cells = jnp.concatenate(
            [
                lax.ppermute(tail, axis, [(i, (i + 1) % count) for i in range(ends)]),
                cells,
                lax.ppermute(head, axis, [((i + 1) % count, i) for i in range(ends)]),
            ],
            axis=dim,
        )
    return cells


def toeplitz(taps, length, radius):
    index = jnp.arange(length, dtype=jnp.int32)
    offset = index[None, :] - index[:, None] + radius
    count = taps.shape[0]
    onehot = (offset[None, :, :] == jnp.arange(count, dtype=jnp.int32)[:, None, None]).astype(
        jnp.float32
    )
    return jnp.sum(onehot * taps[:, None, None], axis=0)


def along_axial(field, matrix):
    flat = field.reshape(-1, field.shape[2])
    out = jnp.dot(flat, matrix, precision=lax.Precision.HIGHEST, preferred_element_type=jnp.float32)
    return out.reshape(field.shape)


def along_second(field, taps, reverse):
    count = taps.shape[0]
    radius = (count - 1) // 2
    length = field.shape[1]
    padded = jnp.pad(field, ((0, 0), (radius, radius), (0, 0)))
    total = jnp.zeros(field.shape, jnp.float32)
    for tap in range(count):
        start = tap if reverse else 2 * radius - tap
        total = total + taps[tap] * padded[:, start : start + length, :]
    return total


def along_first(padded, taps, reverse):
    count = taps.shape[0]
    radius = (count - 1) // 2
    length = padded.shape[0] - 2 * radius
    total = jnp.zeros((length,) + padded.shape[1:], jnp.float32)
    for tap in range(count):
        start = tap if reverse else 2 * radius - tap
        total = total + taps[tap] * padded[start : start + length]
    return total


def spread(piece):
    return lax.all_gather(piece, "view", axis=1, tiled=True)


def local(estimate, images, taps_first, taps_second, taps_axial):
    first = taps_first[0]
    second = taps_second[0]
    axial = taps_axial[0]
    image = images[0]
    radius = (first.shape[0] - 1) // 2
    matrix = toeplitz(axial, estimate.shape[2], (axial.shape[0] - 1) // 2)
    views = lax.axis_size("view")
    width = estimate.shape[1]
    current = spread(estimate)
    for step in range(ITERS):
        inner = along_second(along_axial(current, matrix), second, False)
        blurred = along_first(extended(inner, (("tile", 0),), radius), first, False)
        ratio = image / blurred
        inner = along_second(along_axial(ratio, matrix.T), second, True)
        total = along_first(extended(inner, (("tile", 0),), radius), first, True)
        current = current * (lax.psum(total, "view") / views)
    own = lax.dynamic_slice_in_dim(current, lax.axis_index("view") * width, width, 1)
    return own


def solution(mesh):
    in_specs = (
        P("tile", "view", None),
        P("view", "tile", None, None),
        P("view", None),
        P("view", None),
        P("view", None),
    )
    out_specs = P("tile", "view", None)
    return jax.shard_map(local, mesh=mesh, in_specs=in_specs, out_specs=out_specs, check_vma=False)
```

profile of v0, /device:TPU:2, one launch (start us, length us, event | category | flops | bytes accessed | tf_op | source)
XLA Modules:
  0.0 563.0 jit_solution(5084498150551239331)
XLA Ops:
  9.8 90.1 %all-gather.2.cloned.1.call-done = f32[8,256,128]{2,1,0:T(8,128)} async-done(((f32[8,16,128]{2,1,0:T(8,128)}), f32[8,256,128]{2,1,0:T(8,128)}) %all-gather.2.cloned.1.call-update) | async-done | bytes 1048592 | tf_op jit(solution)/shard_map/all_gather | solution.py:66
  99.9 2.3 convolution_bitcast_fusion
  102.5 5.0 multiply_add_fusion.3
  107.7 2.1 collective-permute-start
  109.7 2.4 collective-permute-start.1
  112.8 3.1 collective-permute-done
  115.9 10.1 %collective-permute-done.1 = f32[2,256,128]{2,1,0:T(8,128)S(1)} collective-permute-done((f32[2,256,128]{2,1,0:T(8,128)S(1)}, f32[2,256,128]{2,1,0:T(8,128)S(1)}, u32[]{:S(2)}, u32[]{:S(2)}) %collective-permute-start.1) | collective-permute-done | bytes 262176 | tf_op jit(solution)/shard_map/ppermute | solution.py:17
  126.0 4.4 fusion.54
  130.5 5.0 multiply_add_fusion.2
  137.5 8.4 %collective-permute-start.3 = (f32[2,256,128]{2,1,0:T(8,128)S(1)}, f32[2,256,128]{2,1,0:T(8,128)S(1)}, u32[]{:S(2)}, u32[]{:S(2)}) collective-permute-start(f32[2,256,128]{2,1,0:T(8,128)S(1)} %get-tuple-element.10), channel_id=1, source_target_pairs={{1,0},{2,1},{3,2},{4,3},{5,4},{6,5},{7,6},{8,7},{9,8},{10,9},{11,1... | collective-permute-start | bytes 786440 | tf_op jit(solution)/shard_map/ppermute | solution.py:19
  146.0 4.2 collective-permute-done.2
  151.9 4.5 fusion.20
  156.4 171.3 %all-reduce.7.cloned.1.call-done = f32[8,256,128]{2,1,0:T(8,128)} async-done(((f32[8,256,128]{2,1,0:T(8,128)}), f32[8,256,128]{2,1,0:T(8,128)}) %all-reduce.7.cloned.1.call-update) | async-done | bytes 1048592 | tf_op jit(solution)/shard_map/psum | solution.py:85
  330.1 5.0 multiply_add_fusion.1
  337.1 2.4 collective-permute-start.5
  339.5 4.1 collective-permute-done.4
  343.6 9.3 %collective-permute-done.5 = f32[2,256,128]{2,1,0:T(8,128)S(1)} collective-permute-done((f32[2,256,128]{2,1,0:T(8,128)S(1)}, f32[2,256,128]{2,1,0:T(8,128)S(1)}, u32[]{:S(2)}, u32[]{:S(2)}) %collective-permute-start.5) | collective-permute-done | bytes 262176 | tf_op jit(solution)/shard_map/ppermute | solution.py:17
  352.9 4.4 fusion.56
  357.3 5.0 multiply_add_fusion
  364.3 8.4 %collective-permute-start.7 = (f32[2,256,128]{2,1,0:T(8,128)S(1)}, f32[2,256,128]{2,1,0:T(8,128)S(1)}, u32[]{:S(2)}, u32[]{:S(2)}) collective-permute-start(f32[2,256,128]{2,1,0:T(8,128)S(1)} %get-tuple-element.6), channel_id=1, source_target_pairs={{1,0},{2,1},{3,2},{4,3},{5,4},{6,5},{7,6},{8,7},{9,8},{10,9},{11,1... | collective-permute-start | bytes 786440 | tf_op jit(solution)/shard_map/ppermute | solution.py:19
  372.8 3.8 collective-permute-done.6
  376.6 3.8 collective-permute-done.7
  380.4 4.5 fusion.3
  384.9 170.1 %all-reduce.9.cloned.1.call-done = f32[8,256,128]{2,1,0:T(8,128)} async-done(((f32[8,256,128]{2,1,0:T(8,128)}), f32[8,256,128]{2,1,0:T(8,128)}) %all-reduce.9.cloned.1.call-update) | async-done | bytes 1048592 | tf_op jit(solution)/shard_map/psum | solution.py:85
  (28 shorter events, 15.7 us)
Async XLA Ops:
  6.5 93.4 %all-gather.2.cloned.1.call-start = ((), (), s32[]{:S(2)}) async-start(), calls=%async_computation | async-start | bytes 1114112 | tf_op jit(solution)/shard_map/all_gather | solution.py:66
  7.3 320.5 %all-reduce.7.cloned.1.call-start = ((), (), s32[]{:S(2)}) async-start(), calls=%async_computation.1 | async-start | bytes 2097152 | tf_op jit(solution)/shard_map/psum | solution.py:85
  107.6 4.5 copy-start.1
  107.6 18.4 %copy-start.2 = (f32[1,8,256,128]{3,2,1,0:T(8,128)S(1)}, f32[1,8,256,128]{3,2,1,0:T(8,128)}, u32[]{:S(2)}) copy-start(f32[1,8,256,128]{3,2,1,0:T(8,128)} %param.6) | copy-start | bytes 3145732
  107.7 8.3 %collective-permute-start = (f32[2,256,128]{2,1,0:T(8,128)S(1)}, f32[2,256,128]{2,1,0:T(8,128)S(1)}, u32[]{:S(2)}, u32[]{:S(2)}) collective-permute-start(f32[2,256,128]{2,1,0:T(8,128)S(1)} %get-tuple-element.11), channel_id=1, source_target_pairs={{1,0},{2,1},{3,2},{4,3},{5,4},{6,5},{7,6},{8,7},{9,8},{10,9},{11,1... | collective-permute-start | bytes 786440 | tf_op jit(solution)/shard_map/ppermute | solution.py:19
  109.7 16.3 %collective-permute-start.1 = (f32[2,256,128]{2,1,0:T(8,128)S(1)}, f32[2,256,128]{2,1,0:T(8,128)S(1)}, u32[]{:S(2)}, u32[]{:S(2)}) collective-permute-start(f32[2,256,128]{2,1,0:T(8,128)S(1)} %get-tuple-element.12), channel_id=1, source_target_pairs={{0,1},{1,2},{2,3},{3,4},{4,5},{5,6},{6,7},{7,8},{8,9},{9,10},{10,1... | collective-permute-start | bytes 786440 | tf_op jit(solution)/shard_map/ppermute | solution.py:17
  135.6 14.6 %collective-permute-start.2 = (f32[2,256,128]{2,1,0:T(8,128)S(1)}, f32[2,256,128]{2,1,0:T(8,128)S(1)}, u32[]{:S(2)}, u32[]{:S(2)}) collective-permute-start(f32[2,256,128]{2,1,0:T(8,128)S(1)} %get-tuple-element.9), channel_id=1, source_target_pairs={{0,1},{1,2},{2,3},{3,4},{4,5},{5,6},{6,7},{7,8},{8,9},{9,10},{10,1... | collective-permute-start | bytes 786440 | tf_op jit(solution)/shard_map/ppermute | solution.py:17
  137.5 14.4 %collective-permute-start.3 = (f32[2,256,128]{2,1,0:T(8,128)S(1)}, f32[2,256,128]{2,1,0:T(8,128)S(1)}, u32[]{:S(2)}, u32[]{:S(2)}) collective-permute-start(f32[2,256,128]{2,1,0:T(8,128)S(1)} %get-tuple-element.10), channel_id=1, source_target_pairs={{1,0},{2,1},{3,2},{4,3},{5,4},{6,5},{7,6},{8,7},{9,8},{10,9},{11,1... | collective-permute-start | bytes 786440 | tf_op jit(solution)/shard_map/ppermute | solution.py:19
  156.4 171.4 %copy-start = (f32[8,256,128]{2,1,0:T(8,128)S(1)}, f32[8,256,128]{2,1,0:T(8,128)}, u32[]{:S(2)}) copy-start(f32[8,256,128]{2,1,0:T(8,128)} %all-gather.2.cloned.1.call-done) | copy-start | bytes 3145732
  156.4 398.6 %all-reduce.9.cloned.1.call-start = ((), (), s32[]{:S(2)}) async-start(), calls=%async_computation.2 | async-start | bytes 2097152 | tf_op jit(solution)/shard_map/psum | solution.py:85
  335.2 8.4 %collective-permute-start.4 = (f32[2,256,128]{2,1,0:T(8,128)S(1)}, f32[2,256,128]{2,1,0:T(8,128)S(1)}, u32[]{:S(2)}, u32[]{:S(2)}) collective-permute-start(f32[2,256,128]{2,1,0:T(8,128)S(1)} %get-tuple-element.7), channel_id=1, source_target_pairs={{1,0},{2,1},{3,2},{4,3},{5,4},{6,5},{7,6},{8,7},{9,8},{10,9},{11,1... | collective-permute-start | bytes 786440 | tf_op jit(solution)/shard_map/ppermute | solution.py:19
  337.1 15.8 %collective-permute-start.5 = (f32[2,256,128]{2,1,0:T(8,128)S(1)}, f32[2,256,128]{2,1,0:T(8,128)S(1)}, u32[]{:S(2)}, u32[]{:S(2)}) collective-permute-start(f32[2,256,128]{2,1,0:T(8,128)S(1)} %get-tuple-element.8), channel_id=1, source_target_pairs={{0,1},{1,2},{2,3},{3,4},{4,5},{5,6},{6,7},{7,8},{8,9},{9,10},{10,1... | collective-permute-start | bytes 786440 | tf_op jit(solution)/shard_map/ppermute | solution.py:17
  362.4 14.2 %collective-permute-start.6 = (f32[2,256,128]{2,1,0:T(8,128)S(1)}, f32[2,256,128]{2,1,0:T(8,128)S(1)}, u32[]{:S(2)}, u32[]{:S(2)}) collective-permute-start(f32[2,256,128]{2,1,0:T(8,128)S(1)} %get-tuple-element.5), channel_id=1, source_target_pairs={{0,1},{1,2},{2,3},{3,4},{4,5},{5,6},{6,7},{7,8},{8,9},{9,10},{10,1... | collective-permute-start | bytes 786440 | tf_op jit(solution)/shard_map/ppermute | solution.py:17
  364.3 16.1 %collective-permute-start.7 = (f32[2,256,128]{2,1,0:T(8,128)S(1)}, f32[2,256,128]{2,1,0:T(8,128)S(1)}, u32[]{:S(2)}, u32[]{:S(2)}) collective-permute-start(f32[2,256,128]{2,1,0:T(8,128)S(1)} %get-tuple-element.6), channel_id=1, source_target_pairs={{1,0},{2,1},{3,2},{4,3},{5,4},{6,5},{7,6},{8,7},{9,8},{10,9},{11,1... | collective-permute-start | bytes 786440 | tf_op jit(solution)/shard_map/ppermute | solution.py:19
Sparse Core Ops, SparseCore 0:
  9.4 90.4 all-gather.1
  156.5 171.2 all-reduce.6
  385.0 169.9 all-reduce.8
where the time goes:
time: 564 us; the launch traced here: 563 us
  waiting for transfers between devices  472 us (84%)
  other arithmetic  32.9 us (6%)
  starting transfers between devices  29.6 us (5%)
  between operations  13.3 us (2%)
  matrix products  12.1 us (2%)
    psum x2, waiting for transfers between devices, local(): current = current * (lax.psum(total, 'view') / views)  341 us
    all_gather x1, waiting for transfers between devices, spread(): return lax.all_gather(piece, 'view', axis=1, tiled=True)  90.1 us
    ppermute x4, waiting for transfers between devices, extended(): lax.ppermute(tail, axis, [(i, (i + 1) % count) for i in range(ends)])  27.3 us
    ppermute x4, starting transfers between devices, extended(): lax.ppermute(head, axis, [((i + 1) % count, i) for i in range(ends)])  20.9 us
    add x4, other arithmetic, along_second(): total = total + taps[tap] * padded[:, start:start + length, :]  20.2 us
    ppermute x4, waiting for transfers between devices, extended(): lax.ppermute(head, axis, [((i + 1) % count, i) for i in range(ends)])  12.8 us
    dot_general x4, matrix products, along_axial(): jnp.dot(flat, matrix, precision=lax.Precision.HIGHEST, preferred_element_...  12.1 us
  transfers between devices with their start and end apart: 11, of which 11 were waited for; matrix products, arithmetic and copies ran while one was open for 1% of the time, Pallas kernels for 0%

commit v1 on v0

--- a/solution.py
+++ b/solution.py
@@ -63,7 +63,9 @@
 
 
 def spread(piece):
-    return lax.all_gather(piece, "view", axis=1, tiled=True)
+    return jnp.concatenate(
+        lax.all_to_all(jnp.stack([piece] * lax.axis_size("view")), "view", 0, 0), axis=1
+    )
 
 
 def local(estimate, images, taps_first, taps_second, taps_axial):

time: 564 us -> 518 us (0.918)
  waiting for transfers between devices: 472 us -> 413 us
  starting transfers between devices: 29.6 us -> 42.9 us
    all_gather x1 -> x0, waiting for transfers between devices: 90.1 us -> none  [spread(): return lax.all_gather(piece, 'view', axis=1, tiled=True)]
    all_to_all x0 -> x1, waiting for transfers between devices: none -> 23.5 us  [spread(): lax.all_to_all(jnp.stack([piece] * lax.axis_size('view')), 'view', 0, 0)]
    psum x2, waiting for transfers between devices: 341 us -> 354 us  [local(): current = current * (lax.psum(total, 'view') / views)]
    all_to_all x0 -> x1, starting transfers between devices: none -> 8.77 us  [spread(): lax.all_to_all(jnp.stack([piece] * lax.axis_size('view')), 'view', 0, 0)]
  transfers between devices with their start and end apart: 11 -> 11, of which waited for: 11 -> 11; matrix products, arithmetic and copies ran while one was open for 1% -> 0% of each run, Pallas kernels for 0% -> 0%
where the time goes in v1:
time: 518 us; the launch traced here: 517 us
  waiting for transfers between devices  413 us (80%)
  starting transfers between devices  42.9 us (8%)
  other arithmetic  33 us (6%)
  between operations  13.6 us (3%)
  matrix products  10.9 us (2%)
    psum x2, waiting for transfers between devices, local(): current = current * (lax.psum(total, 'view') / views)  354 us
    ppermute x4, starting transfers between devices, extended(): lax.ppermute(head, axis, [((i + 1) % count, i) for i in range(ends)])  25.9 us
    ppermute x4, waiting for transfers between devices, extended(): lax.ppermute(tail, axis, [(i, (i + 1) % count) for i in range(ends)])  23.9 us
    all_to_all x1, waiting for transfers between devices, spread(): lax.all_to_all(jnp.stack([piece] * lax.axis_size('view')), 'view', 0, 0)  23.5 us
    add x4, other arithmetic, along_second(): total = total + taps[tap] * padded[:, start:start + length, :]  20.9 us
    ppermute x4, waiting for transfers between devices, extended(): lax.ppermute(head, axis, [((i + 1) % count, i) for i in range(ends)])  10.9 us
    dot_general x4, matrix products, along_axial(): jnp.dot(flat, matrix, precision=lax.Precision.HIGHEST, preferred_element_...  10.9 us
  transfers between devices with their start and end apart: 11, of which 11 were waited for; matrix products, arithmetic and copies ran while one was open for 0% of the time, Pallas kernels for 0%

profile of v1, /device:TPU:2, one launch (start us, length us, event | category | flops | bytes accessed | tf_op | source)
XLA Modules:
  0.0 517.0 jit_solution(2804108270566694373)
XLA Ops:
  6.5 1.9 stack.2
  8.5 8.8 %all-to-all-start = ((f32[16,8,16,128]{3,2,1,0:T(8,128)}), f32[16,8,16,128]{3,2,1,0:T(8,128)S(1)}, u32[]{:S(2)}, u32[]{:S(2)}) async-start(f32[16,8,16,128]{3,2,1,0:T(8,128)} %stack.2), calls=%async_computation | async-start | bytes 2097152 | tf_op jit(solution)/shard_map/all_to_all | solution.py:67
  18.3 23.5 %all-to-all-done = f32[16,8,16,128]{3,2,1,0:T(8,128)S(1)} async-done(((f32[16,8,16,128]{3,2,1,0:T(8,128)}), f32[16,8,16,128]{3,2,1,0:T(8,128)S(1)}, u32[]{:S(2)}, u32[]{:S(2)}) %all-to-all-start) | async-done | bytes 1048608 | tf_op jit(solution)/shard_map/all_to_all | solution.py:67
  43.3 5.2 %multiply_add_fusion.3 = f32[8,256,128]{2,1,0:T(8,128)S(1)} fusion(f32[8,256,128]{2,1,0:T(8,128)S(1)} %bitcast.38, f32[]{:T(128)} %bitcast.13, f32[]{:T(128)} %bitcast.12, f32[]{:T(128)} %bitcast.11, f32[]{:T(128)} %bitcast.10, f32[]{:T(128)} %bitcast.9, f32[]{:T(128)} %bitcast.8, f32[]{:T(128)} %bitcast.3), kind=kLoop, calls=%fused_computation.88 | loop fusion | flops 3407872 | bytes 2097180 | tf_op jit(solution)/shard_map/add | solution.py:50
  48.6 7.1 %collective-permute-start = (f32[2,256,128]{2,1,0:T(8,128)S(1)}, f32[2,256,128]{2,1,0:T(8,128)S(1)}, u32[]{:S(2)}, u32[]{:S(2)}) collective-permute-start(f32[2,256,128]{2,1,0:T(8,128)S(1)} %get-tuple-element.11), channel_id=1, source_target_pairs={{1,0},{2,1},{3,2},{4,3},{5,4},{6,5},{7,6},{8,7},{9,8},{10,9},{11,1... | collective-permute-start | bytes 786440 | tf_op jit(solution)/shard_map/ppermute | solution.py:19
  59.6 8.8 %collective-permute-done.1 = f32[2,256,128]{2,1,0:T(8,128)S(1)} collective-permute-done((f32[2,256,128]{2,1,0:T(8,128)S(1)}, f32[2,256,128]{2,1,0:T(8,128)S(1)}, u32[]{:S(2)}, u32[]{:S(2)}) %collective-permute-start.1) | collective-permute-done | bytes 262176 | tf_op jit(solution)/shard_map/ppermute | solution.py:17
  68.4 4.4 fusion.54
  72.8 5.2 %multiply_add_fusion.2 = f32[8,256,128]{2,1,0:T(8,128)S(1)} fusion(f32[8,256,128]{2,1,0:T(8,128)S(1)} %fusion.54, f32[]{:T(128)} %bitcast.13, f32[]{:T(128)} %bitcast.12, f32[]{:T(128)} %bitcast.11, f32[]{:T(128)} %bitcast.10, f32[]{:T(128)} %bitcast.9, f32[]{:T(128)} %bitcast.8, f32[]{:T(128)} %bitcast.3), kind=kLoop, calls=%fused_computation.82 | loop fusion | flops 3407872 | bytes 2097180 | tf_op jit(solution)/shard_map/add | solution.py:50
  80.0 8.4 %collective-permute-start.3 = (f32[2,256,128]{2,1,0:T(8,128)S(1)}, f32[2,256,128]{2,1,0:T(8,128)S(1)}, u32[]{:S(2)}, u32[]{:S(2)}) collective-permute-start(f32[2,256,128]{2,1,0:T(8,128)S(1)} %get-tuple-element.10), channel_id=1, source_target_pairs={{1,0},{2,1},{3,2},{4,3},{5,4},{6,5},{7,6},{8,7},{9,8},{10,9},{11,1... | collective-permute-start | bytes 786440 | tf_op jit(solution)/shard_map/ppermute | solution.py:19
  88.5 2.1 collective-permute-done.2
  92.3 4.5 fusion.20
  96.9 184.2 %all-reduce.7.cloned.1.call-done = f32[8,256,128]{2,1,0:T(8,128)} async-done(((f32[8,256,128]{2,1,0:T(8,128)}), f32[8,256,128]{2,1,0:T(8,128)}) %all-reduce.7.cloned.1.call-update) | async-done | bytes 1048592 | tf_op jit(solution)/shard_map/psum | solution.py:87
  283.5 5.2 %multiply_add_fusion.1 = f32[8,256,128]{2,1,0:T(8,128)S(1)} fusion(f32[8,256,128]{2,1,0:T(8,128)S(1)} %fusion.69, f32[]{:T(128)} %bitcast.13, f32[]{:T(128)} %bitcast.12, f32[]{:T(128)} %bitcast.11, f32[]{:T(128)} %bitcast.10, f32[]{:T(128)} %bitcast.9, f32[]{:T(128)} %bitcast.8, f32[]{:T(128)} %bitcast.3), kind=kLoop, calls=%fused_computation.76 | loop fusion | flops 3407872 | bytes 2097180 | tf_op jit(solution)/shard_map/add | solution.py:50
  288.7 1.9 collective-permute-start.4
  290.7 2.4 collective-permute-start.5
  293.1 4.1 collective-permute-done.4
  297.2 9.3 %collective-permute-done.5 = f32[2,256,128]{2,1,0:T(8,128)S(1)} collective-permute-done((f32[2,256,128]{2,1,0:T(8,128)S(1)}, f32[2,256,128]{2,1,0:T(8,128)S(1)}, u32[]{:S(2)}, u32[]{:S(2)}) %collective-permute-start.5) | collective-permute-done | bytes 262176 | tf_op jit(solution)/shard_map/ppermute | solution.py:17
  306.4 4.4 fusion.56
  310.9 5.2 %multiply_add_fusion = f32[8,256,128]{2,1,0:T(8,128)S(1)} fusion(f32[8,256,128]{2,1,0:T(8,128)S(1)} %fusion.56, f32[]{:T(128)} %bitcast.13, f32[]{:T(128)} %bitcast.12, f32[]{:T(128)} %bitcast.11, f32[]{:T(128)} %bitcast.10, f32[]{:T(128)} %bitcast.9, f32[]{:T(128)} %bitcast.8, f32[]{:T(128)} %bitcast.3), kind=kLoop, calls=%fused_computation.70 | loop fusion | flops 3407872 | bytes 2097180 | tf_op jit(solution)/shard_map/add | solution.py:50
  318.1 8.4 %collective-permute-start.7 = (f32[2,256,128]{2,1,0:T(8,128)S(1)}, f32[2,256,128]{2,1,0:T(8,128)S(1)}, u32[]{:S(2)}, u32[]{:S(2)}) collective-permute-start(f32[2,256,128]{2,1,0:T(8,128)S(1)} %get-tuple-element.6), channel_id=1, source_target_pairs={{1,0},{2,1},{3,2},{4,3},{5,4},{6,5},{7,6},{8,7},{9,8},{10,9},{11,1... | collective-permute-start | bytes 786440 | tf_op jit(solution)/shard_map/ppermute | solution.py:19
  326.5 3.8 collective-permute-done.6
  330.3 3.9 collective-permute-done.7
  334.1 4.5 fusion.3
  338.7 170.0 %all-reduce.9.cloned.1.call-done = f32[8,256,128]{2,1,0:T(8,128)} async-done(((f32[8,256,128]{2,1,0:T(8,128)}), f32[8,256,128]{2,1,0:T(8,128)}) %all-reduce.9.cloned.1.call-update) | async-done | bytes 1048592 | tf_op jit(solution)/shard_map/psum | solution.py:87
  (31 shorter events, 16.0 us)
Async XLA Ops:
  8.5 8.8 %copy-start = (f32[1,7]{1,0:T(1,128)S(1)}, f32[1,7]{1,0:T(1,128)}, u32[]{:S(2)}) copy-start(f32[1,7]{1,0:T(1,128)} %param.8) | copy-start | bytes 88
  8.5 9.5 %copy-start.2 = (f32[1,33]{1,0:T(1,128)S(1)}, f32[1,33]{1,0:T(1,128)}, u32[]{:S(2)}) copy-start(f32[1,33]{1,0:T(1,128)} %param.9) | copy-start | bytes 400
  8.5 33.3 %all-to-all-start = ((f32[16,8,16,128]{3,2,1,0:T(8,128)}), f32[16,8,16,128]{3,2,1,0:T(8,128)S(1)}, u32[]{:S(2)}, u32[]{:S(2)}) async-start(f32[16,8,16,128]{3,2,1,0:T(8,128)} %stack.2), calls=%async_computation | async-start | bytes 2097152 | tf_op jit(solution)/shard_map/all_to_all | solution.py:67
  17.2 263.9 %all-reduce.7.cloned.1.call-start = ((), (), s32[]{:S(2)}) async-start(), calls=%async_computation.1 | async-start | bytes 2097152 | tf_op jit(solution)/shard_map/psum | solution.py:87
  48.6 9.1 %copy-start.1 = (f32[1,5]{1,0:T(1,128)S(1)}, f32[1,5]{1,0:T(1,128)}, u32[]{:S(2)}) copy-start(f32[1,5]{1,0:T(1,128)} %param.7) | copy-start | bytes 64
  48.6 19.8 %copy-start.3 = (f32[1,8,256,128]{3,2,1,0:T(8,128)S(1)}, f32[1,8,256,128]{3,2,1,0:T(8,128)}, u32[]{:S(2)}) copy-start(f32[1,8,256,128]{3,2,1,0:T(8,128)} %param.6) | copy-start | bytes 3145732
  48.6 11.0 %collective-permute-start = (f32[2,256,128]{2,1,0:T(8,128)S(1)}, f32[2,256,128]{2,1,0:T(8,128)S(1)}, u32[]{:S(2)}, u32[]{:S(2)}) collective-permute-start(f32[2,256,128]{2,1,0:T(8,128)S(1)} %get-tuple-element.11), channel_id=1, source_target_pairs={{1,0},{2,1},{3,2},{4,3},{5,4},{6,5},{7,6},{8,7},{9,8},{10,9},{11,1... | collective-permute-start | bytes 786440 | tf_op jit(solution)/shard_map/ppermute | solution.py:19
  55.7 12.6 %collective-permute-start.1 = (f32[2,256,128]{2,1,0:T(8,128)S(1)}, f32[2,256,128]{2,1,0:T(8,128)S(1)}, u32[]{:S(2)}, u32[]{:S(2)}) collective-permute-start(f32[2,256,128]{2,1,0:T(8,128)S(1)} %get-tuple-element.12), channel_id=1, source_target_pairs={{0,1},{1,2},{2,3},{3,4},{4,5},{5,6},{6,7},{7,8},{8,9},{9,10},{10,1... | collective-permute-start | bytes 786440 | tf_op jit(solution)/shard_map/ppermute | solution.py:17
  78.1 12.5 %collective-permute-start.2 = (f32[2,256,128]{2,1,0:T(8,128)S(1)}, f32[2,256,128]{2,1,0:T(8,128)S(1)}, u32[]{:S(2)}, u32[]{:S(2)}) collective-permute-start(f32[2,256,128]{2,1,0:T(8,128)S(1)} %get-tuple-element.9), channel_id=1, source_target_pairs={{0,1},{1,2},{2,3},{3,4},{4,5},{5,6},{6,7},{7,8},{8,9},{9,10},{10,1... | collective-permute-start | bytes 786440 | tf_op jit(solution)/shard_map/ppermute | solution.py:17
  80.0 12.3 %collective-permute-start.3 = (f32[2,256,128]{2,1,0:T(8,128)S(1)}, f32[2,256,128]{2,1,0:T(8,128)S(1)}, u32[]{:S(2)}, u32[]{:S(2)}) collective-permute-start(f32[2,256,128]{2,1,0:T(8,128)S(1)} %get-tuple-element.10), channel_id=1, source_target_pairs={{1,0},{2,1},{3,2},{4,3},{5,4},{6,5},{7,6},{8,7},{9,8},{10,9},{11,1... | collective-permute-start | bytes 786440 | tf_op jit(solution)/shard_map/ppermute | solution.py:19
  96.8 411.8 %all-reduce.9.cloned.1.call-start = ((), (), s32[]{:S(2)}) async-start(), calls=%async_computation.2 | async-start | bytes 2097152 | tf_op jit(solution)/shard_map/psum | solution.py:87
  288.7 8.4 %collective-permute-start.4 = (f32[2,256,128]{2,1,0:T(8,128)S(1)}, f32[2,256,128]{2,1,0:T(8,128)S(1)}, u32[]{:S(2)}, u32[]{:S(2)}) collective-permute-start(f32[2,256,128]{2,1,0:T(8,128)S(1)} %get-tuple-element.7), channel_id=1, source_target_pairs={{1,0},{2,1},{3,2},{4,3},{5,4},{6,5},{7,6},{8,7},{9,8},{10,9},{11,1... | collective-permute-start | bytes 786440 | tf_op jit(solution)/shard_map/ppermute | solution.py:19
  290.7 15.8 %collective-permute-start.5 = (f32[2,256,128]{2,1,0:T(8,128)S(1)}, f32[2,256,128]{2,1,0:T(8,128)S(1)}, u32[]{:S(2)}, u32[]{:S(2)}) collective-permute-start(f32[2,256,128]{2,1,0:T(8,128)S(1)} %get-tuple-element.8), channel_id=1, source_target_pairs={{0,1},{1,2},{2,3},{3,4},{4,5},{5,6},{6,7},{7,8},{8,9},{9,10},{10,1... | collective-permute-start | bytes 786440 | tf_op jit(solution)/shard_map/ppermute | solution.py:17
  316.1 14.1 %collective-permute-start.6 = (f32[2,256,128]{2,1,0:T(8,128)S(1)}, f32[2,256,128]{2,1,0:T(8,128)S(1)}, u32[]{:S(2)}, u32[]{:S(2)}) collective-permute-start(f32[2,256,128]{2,1,0:T(8,128)S(1)} %get-tuple-element.5), channel_id=1, source_target_pairs={{0,1},{1,2},{2,3},{3,4},{4,5},{5,6},{6,7},{7,8},{8,9},{9,10},{10,1... | collective-permute-start | bytes 786440 | tf_op jit(solution)/shard_map/ppermute | solution.py:17
  318.1 16.1 %collective-permute-start.7 = (f32[2,256,128]{2,1,0:T(8,128)S(1)}, f32[2,256,128]{2,1,0:T(8,128)S(1)}, u32[]{:S(2)}, u32[]{:S(2)}) collective-permute-start(f32[2,256,128]{2,1,0:T(8,128)S(1)} %get-tuple-element.6), channel_id=1, source_target_pairs={{1,0},{2,1},{3,2},{4,3},{5,4},{6,5},{7,6},{8,7},{9,8},{10,9},{11,1... | collective-permute-start | bytes 786440 | tf_op jit(solution)/shard_map/ppermute | solution.py:19
Sparse Core Ops, SparseCore 0:
  97.0 184.1 all-reduce.6
  338.8 169.8 all-reduce.8
